TPU v7x, 512 devices: a whole 4x8x8 slice. The times are simulated.
512 devices in a mesh: shard: 128 (over z, y, core), rep: 4 (over x).
Axes of the slice: x: 4, y: 8, z: 8, core: 2. Of those that a mesh axis runs over, the one named last changes fastest.
Arguments:
- embeddings: bfloat16 [262144, 1024], P('shard'), may hold values from -200 to 200
- labels: int32 [262144], P('shard'), may hold values from 0 to 255, never falling along the last dimension, each value on 1 to 8193 neighbouring positions
Outputs:
- best_similarity: float32 [262144], P('shard')
Inputs may be any that keep to these rules, and one draw needn't show every extreme that they name: labels never fall along the rows; each cluster holds at most 8193 consecutive rows, and one cluster holds exactly that many.
All inputs are finite; a program needn't handle non-finite values.
Results may differ from a plain program's by a relative error of at most 0.00063.
Values may be sent and summed in bfloat16 or wider, within the bound.
A program may use at most 64 MiB of HBM per device.

v0:
```python
import math

import jax
import jax.numpy as jnp
from jax import lax
from jax.sharding import PartitionSpec as P

LOOK = 4


def shifted(block, axis, distance):
    devices = range(lax.axis_size(axis))
    route = [(i - distance, i) for i in devices if i - distance in devices]
    return lax.ppermute(block, axis, route)


def normalize(values):
    as_float = values.astype(jnp.float32)
    inverse = lax.rsqrt(jnp.mean(as_float * as_float, axis=1, keepdims=True) + 1e-06)
    return (as_float * inverse / math.sqrt(values.shape[1])).astype(jnp.bfloat16)


def compare(queries, query_labels, query_pos, keys, key_labels, key_pos, current):
    scores = lax.dot_general(
        queries, keys, (((1,), (1,)), ((), ())), preferred_element_type=jnp.float32
    )
    keep = (key_labels[None, :] == query_labels[:, None]) & (key_pos[None, :] < query_pos[:, None])
    return jnp.maximum(current, jnp.max(jnp.where(keep, scores, jnp.float32(-1.0)), axis=1))


def fetch(sent_piece, offset_dev):
    result = shifted((sent_piece[0], sent_piece[1]), "shard", offset_dev)
    return result


def local(embeddings, labels):
    tok_rows = embeddings.shape[0]
    rep_count = lax.axis_size("rep")
    device = lax.axis_index("shard")
    replica = lax.axis_index("rep")
    unit_rows = normalize(embeddings)
    positions = device * tok_rows + jnp.arange(tok_rows, dtype=jnp.int32)
    quarter = tok_rows // rep_count
    start_row = replica * quarter
    queries, query_labels, query_pos = (unit_rows, labels, positions)
    sent_piece = (
        lax.dynamic_slice_in_dim(unit_rows, start_row, quarter, 0),
        lax.dynamic_slice_in_dim(labels, start_row, quarter, 0),
    )
    offsets = start_row + jnp.arange(quarter, dtype=jnp.int32)
    best_sim = jnp.full((queries.shape[0],), -1.0, jnp.float32)
    best_sim = compare(
        queries,
        query_labels,
        query_pos,
        sent_piece[0],
        sent_piece[1],
        device * tok_rows + offsets,
        best_sim,
    )
    carried = sent_piece
    for offset_dev in range(1, LOOK + 1):
        carried = fetch(sent_piece, offset_dev)
        key_pos = (device - offset_dev) * tok_rows + offsets
        key_pos = jnp.where(device >= offset_dev, key_pos, jnp.int32(2**30))
        best_sim = compare(
            queries, query_labels, query_pos, carried[0], carried[1], key_pos, best_sim
        )
    merged = lax.pmax(best_sim, "rep")
    return merged


def solution(mesh):
    placed = (P("shard", None), P("shard"))
    return jax.shard_map(local, mesh=mesh, in_specs=placed, out_specs=P("shard"), check_vma=False)
```

profile of v0, /device:TPU:256, one launch (start us, length us, event | category | flops | bytes accessed | tf_op | source)
XLA Modules:
  0.0 164.2 jit_solution(16212158286794161147)
XLA Ops:
  0.0 0.0 copy-start
  0.0 0.9 dynamic_slice.6
  0.9 4.6 %collective-permute-start.6 = (s32[512]{0:T(512)S(1)}, s32[512]{0:T(512)S(1)}, u32[]{:S(2)}, u32[]{:S(2)}) collective-permute-start(s32[512]{0:T(512)S(1)} %dynamic_slice.6), channel_id=1, source_target_pairs={{0,16},{4,20},{8,24},{12,28},{16,32},{20,36},{24,40},{28,44},{32,4... | collective-permute-start | bytes 6152 | tf_op jit(solution)/shard_map/ppermute | solution.py:14
  5.5 2.6 %collective-permute-start.4 = (s32[512]{0:T(512)S(1)}, s32[512]{0:T(512)S(1)}, u32[]{:S(2)}, u32[]{:S(2)}) collective-permute-start(s32[512]{0:T(512)S(1)} %dynamic_slice.6), channel_id=1, source_target_pairs={{0,12},{4,16},{8,20},{12,24},{16,28},{20,32},{24,36},{28,40},{32,4... | collective-permute-start | bytes 6152 | tf_op jit(solution)/shard_map/ppermute | solution.py:14
  8.2 4.7 %collective-permute-start.2 = (s32[512]{0:T(512)S(1)}, s32[512]{0:T(512)S(1)}, u32[]{:S(2)}, u32[]{:S(2)}) collective-permute-start(s32[512]{0:T(512)S(1)} %dynamic_slice.6), channel_id=1, source_target_pairs={{0,8},{4,12},{8,16},{12,20},{16,24},{20,28},{24,32},{28,36},{32,40... | collective-permute-start | bytes 6152 | tf_op jit(solution)/shard_map/ppermute | solution.py:14
  12.9 3.1 %fusion = f32[2048]{0:T(1024)S(1)} fusion(bf16[2048,1024]{1,0:T(8,128)(2,1)} %param.2), kind=kLoop, calls=%fused_computation.2 | loop fusion | flops 6289408 | bytes 4202496 | tf_op jit(solution)/shard_map/reduce_sum | solution.py:19
  16.0 0.0 copy-done
  16.0 0.0 copy-start.3
  16.0 1.1 fusion.2
  17.1 0.0 copy-start.1
  17.1 1.9 %copy-done.1 = bf16[2048,1024]{1,0:T(8,128)(2,1)} copy-done((bf16[2048,1024]{1,0:T(8,128)(2,1)}, bf16[2048,1024]{1,0:T(8,128)(2,1)S(1)}, u32[]{:S(2)}) %copy-start.1) | copy-done | bytes 4194328
  19.1 0.1 constant_dynamic-slice_fusion
  19.1 3.0 %collective-permute-start.5 = (bf16[512,1024]{1,0:T(8,128)(2,1)S(1)}, bf16[512,1024]{1,0:T(8,128)(2,1)S(1)}, u32[]{:S(2)}, u32[]{:S(2)}) collective-permute-start(bf16[512,1024]{1,0:T(8,128)(2,1)S(1)} %constant_dynamic-slice_fusion), channel_id=1, source_target_pairs={{0,12},{4,16},{8,20},{12,24},{16,28},{20,32},{24,36},{28,40},{32,4... | collective-permute-start | bytes 3145736 | tf_op jit(solution)/shard_map/ppermute | solution.py:14
  22.1 2.6 %collective-permute-start.3 = (bf16[512,1024]{1,0:T(8,128)(2,1)S(1)}, bf16[512,1024]{1,0:T(8,128)(2,1)S(1)}, u32[]{:S(2)}, u32[]{:S(2)}) collective-permute-start(bf16[512,1024]{1,0:T(8,128)(2,1)S(1)} %constant_dynamic-slice_fusion), channel_id=1, source_target_pairs={{0,8},{4,12},{8,16},{12,20},{16,24},{20,28},{24,32},{28,36},{32,40... | collective-permute-start | bytes 3145736 | tf_op jit(solution)/shard_map/ppermute | solution.py:14
  24.8 0.0 copy-done.3
  24.8 0.0 copy-start.2
  24.8 4.9 %select_reduce_fusion.4 = f32[2048]{0:T(1024)S(1)} fusion(bf16[2048,1024]{1,0:T(8,128)(2,1)} %copy-done.1, bf16[512,1024]{1,0:T(8,128)(2,1)S(1)} %constant_dynamic-slice_fusion, s32[2048]{0:T(1024)S(1)} %iota_add_fusion, s32[2048]{0:T(1024)S(1)} %copy-done.3, s32[512]{0:T(512)S(1)} %fusion.3, s32[512]{0:T(512)S(1)} %dynamic_slice.6), kind=kOutput, calls=%fused_computation.9 | convolution fusion | flops 2152724480 | bytes 5271552 | tf_op jit(solution)/shard_map/dot_general | solution.py:24
  29.7 54.1 %collective-permute-done.3 = bf16[512,1024]{1,0:T(8,128)(2,1)S(1)} collective-permute-done((bf16[512,1024]{1,0:T(8,128)(2,1)S(1)}, bf16[512,1024]{1,0:T(8,128)(2,1)S(1)}, u32[]{:S(2)}, u32[]{:S(2)}) %collective-permute-start.3) | collective-permute-done | bytes 1048608 | tf_op jit(solution)/shard_map/ppermute | solution.py:14
  83.8 1.9 %collective-permute-start.7 = (bf16[512,1024]{1,0:T(8,128)(2,1)S(1)}, bf16[512,1024]{1,0:T(8,128)(2,1)S(1)}, u32[]{:S(2)}, u32[]{:S(2)}) collective-permute-start(bf16[512,1024]{1,0:T(8,128)(2,1)S(1)} %constant_dynamic-slice_fusion), channel_id=1, source_target_pairs={{0,16},{4,20},{8,24},{12,28},{16,32},{20,36},{24,40},{28,44},{32,4... | collective-permute-start | bytes 3145736 | tf_op jit(solution)/shard_map/ppermute | solution.py:14
  85.7 0.0 copy-done.2
  85.7 2.4 %fusion.4 = f32[2048,512]{0,1:T(8,128)S(1)} fusion(bf16[2048,1024]{1,0:T(8,128)(2,1)S(1)} %copy-done.2, bf16[512,1024]{1,0:T(8,128)(2,1)S(1)} %collective-permute-done.3), kind=kOutput, calls=%fused_computation.20 | convolution fusion | flops 2147483648 | bytes 9437184 | tf_op jit(solution)/shard_map/dot_general | solution.py:24
  88.1 0.0 collective-permute-done.5
  88.1 1.9 %collective-permute-start.1 = (bf16[512,1024]{1,0:T(8,128)(2,1)S(1)}, bf16[512,1024]{1,0:T(8,128)(2,1)S(1)}, u32[]{:S(2)}, u32[]{:S(2)}) collective-permute-start(bf16[512,1024]{1,0:T(8,128)(2,1)S(1)} %constant_dynamic-slice_fusion), channel_id=1, source_target_pairs={{0,4},{4,8},{8,12},{12,16},{16,20},{20,24},{24,28},{28,32},{32,36}... | collective-permute-start | bytes 3145736 | tf_op jit(solution)/shard_map/ppermute | solution.py:14
  90.1 2.4 %fusion.5 = f32[2048,512]{0,1:T(8,128)S(1)} fusion(bf16[2048,1024]{1,0:T(8,128)(2,1)S(1)} %copy-done.2, bf16[512,1024]{1,0:T(8,128)(2,1)S(1)} %collective-permute-done.5), kind=kOutput, calls=%fused_computation.21 | convolution fusion | flops 2147483648 | bytes 9437184 | tf_op jit(solution)/shard_map/dot_general | solution.py:24
  92.4 44.4 %collective-permute-done.7 = bf16[512,1024]{1,0:T(8,128)(2,1)S(1)} collective-permute-done((bf16[512,1024]{1,0:T(8,128)(2,1)S(1)}, bf16[512,1024]{1,0:T(8,128)(2,1)S(1)}, u32[]{:S(2)}, u32[]{:S(2)}) %collective-permute-start.7) | collective-permute-done | bytes 1048608 | tf_op jit(solution)/shard_map/ppermute | solution.py:14
  136.8 2.1 %collective-permute-start = (s32[512]{0:T(512)S(1)}, s32[512]{0:T(512)S(1)}, u32[]{:S(2)}, u32[]{:S(2)}) collective-permute-start(s32[512]{0:T(512)S(1)} %dynamic_slice.6), channel_id=1, source_target_pairs={{0,4},{4,8},{8,12},{12,16},{16,20},{20,24},{24,28},{28,32},{32,36}... | collective-permute-start | bytes 6152 | tf_op jit(solution)/shard_map/ppermute | solution.py:14
  138.9 2.4 %fusion.6 = f32[2048,512]{0,1:T(8,128)S(1)} fusion(bf16[2048,1024]{1,0:T(8,128)(2,1)S(1)} %copy-done.2, bf16[512,1024]{1,0:T(8,128)(2,1)S(1)} %collective-permute-done.7), kind=kOutput, calls=%fused_computation.22 | convolution fusion | flops 2147483648 | bytes 9437184 | tf_op jit(solution)/shard_map/dot_general | solution.py:24
  141.3 0.0 collective-permute-done.6
  141.3 0.0 collective-permute-done.4
  141.3 0.0 collective-permute-done.2
  141.3 3.7 %collective-permute-done = s32[512]{0:T(512)S(1)} collective-permute-done((s32[512]{0:T(512)S(1)}, s32[512]{0:T(512)S(1)}, u32[]{:S(2)}, u32[]{:S(2)}) %collective-permute-start) | collective-permute-done | bytes 2080 | tf_op jit(solution)/shard_map/ppermute | solution.py:14
  145.0 0.0 collective-permute-done.1
  145.0 8.0 %select_reduce_fusion.3 = (f32[2048]{0:T(1024)S(1)}, f32[2048]{0:T(1024)S(1)}, f32[2048]{0:T(1024)S(1)}, f32[2048]{0:T(1024)S(1)}) fusion(s32[2048]{0:T(1024)S(1)} %iota_add_fusion, s32[2048]{0:T(1024)S(1)} %copy-done.3, s32[512]{0:T(512)S(1)} %get-tuple-element.12, s32[512]{0:T(512)S(1)} %collective-permute-done, f32[2048,512]{0,1:T(8,128)S(1)} %fusion.4, ...), kind=kOutput, calls=%fused_computation.8 | convolution fusion | flops 2168446976 | bytes 17891328 | tf_op jit(solution)/shard_map/dot_general | solution.py:24
  153.1 11.2 %pmax.7 = f32[2048]{0:T(1024)} all-reduce(f32[2048]{0:T(1024)S(1)} %maximum_maximum_fusion), channel_id=1, replica_groups=mesh['shard'=128,'rep'=4] {'rep'}, use_global_device_ids=true, to_apply=%region_6.7 | all-reduce | flops 2048 | bytes 16384 | tf_op jit(solution)/shard_map/pmax | solution.py:69
  (6 shorter events, 0.0 us)
Async XLA Ops:
  0.0 16.0 %copy-start = (bf16[2048,1024]{1,0:T(8,128)(2,1)S(1)}, bf16[2048,1024]{1,0:T(8,128)(2,1)}, u32[]{:S(2)}) copy-start(bf16[2048,1024]{1,0:T(8,128)(2,1)} %param.2) | copy-start | bytes 12582916
  0.9 140.4 %collective-permute-start.6 = (s32[512]{0:T(512)S(1)}, s32[512]{0:T(512)S(1)}, u32[]{:S(2)}, u32[]{:S(2)}) collective-permute-start(s32[512]{0:T(512)S(1)} %dynamic_slice.6), channel_id=1, source_target_pairs={{0,16},{4,20},{8,24},{12,28},{16,32},{20,36},{24,40},{28,44},{32,4... | collective-permute-start | bytes 6152 | tf_op jit(solution)/shard_map/ppermute | solution.py:14
  5.5 135.8 %collective-permute-start.4 = (s32[512]{0:T(512)S(1)}, s32[512]{0:T(512)S(1)}, u32[]{:S(2)}, u32[]{:S(2)}) collective-permute-start(s32[512]{0:T(512)S(1)} %dynamic_slice.6), channel_id=1, source_target_pairs={{0,12},{4,16},{8,20},{12,24},{16,28},{20,32},{24,36},{28,40},{32,4... | collective-permute-start | bytes 6152 | tf_op jit(solution)/shard_map/ppermute | solution.py:14
  8.2 133.1 %collective-permute-start.2 = (s32[512]{0:T(512)S(1)}, s32[512]{0:T(512)S(1)}, u32[]{:S(2)}, u32[]{:S(2)}) collective-permute-start(s32[512]{0:T(512)S(1)} %dynamic_slice.6), channel_id=1, source_target_pairs={{0,8},{4,12},{8,16},{12,20},{16,24},{20,28},{24,32},{28,36},{32,40... | collective-permute-start | bytes 6152 | tf_op jit(solution)/shard_map/ppermute | solution.py:14
  16.0 8.8 %copy-start.3 = (s32[2048]{0:T(1024)S(1)}, s32[2048]{0:T(1024)}, u32[]{:S(2)}) copy-start(s32[2048]{0:T(1024)} %param.3) | copy-start | bytes 24580
  17.1 1.9 %copy-start.1 = (bf16[2048,1024]{1,0:T(8,128)(2,1)}, bf16[2048,1024]{1,0:T(8,128)(2,1)S(1)}, u32[]{:S(2)}) copy-start(bf16[2048,1024]{1,0:T(8,128)(2,1)S(1)} %fusion.2) | copy-start | bytes 12582916
  19.1 69.0 %collective-permute-start.5 = (bf16[512,1024]{1,0:T(8,128)(2,1)S(1)}, bf16[512,1024]{1,0:T(8,128)(2,1)S(1)}, u32[]{:S(2)}, u32[]{:S(2)}) collective-permute-start(bf16[512,1024]{1,0:T(8,128)(2,1)S(1)} %constant_dynamic-slice_fusion), channel_id=1, source_target_pairs={{0,12},{4,16},{8,20},{12,24},{16,28},{20,32},{24,36},{28,40},{32,4... | collective-permute-start | bytes 3145736 | tf_op jit(solution)/shard_map/ppermute | solution.py:14
  22.1 61.7 %collective-permute-start.3 = (bf16[512,1024]{1,0:T(8,128)(2,1)S(1)}, bf16[512,1024]{1,0:T(8,128)(2,1)S(1)}, u32[]{:S(2)}, u32[]{:S(2)}) collective-permute-start(bf16[512,1024]{1,0:T(8,128)(2,1)S(1)} %constant_dynamic-slice_fusion), channel_id=1, source_target_pairs={{0,8},{4,12},{8,16},{12,20},{16,24},{20,28},{24,32},{28,36},{32,40... | collective-permute-start | bytes 3145736 | tf_op jit(solution)/shard_map/ppermute | solution.py:14
  24.8 60.9 %copy-start.2 = (bf16[2048,1024]{1,0:T(8,128)(2,1)S(1)}, bf16[2048,1024]{1,0:T(8,128)(2,1)}, u32[]{:S(2)}) copy-start(bf16[2048,1024]{1,0:T(8,128)(2,1)} %copy-done.1) | copy-start | bytes 12582916
  83.8 53.0 %collective-permute-start.7 = (bf16[512,1024]{1,0:T(8,128)(2,1)S(1)}, bf16[512,1024]{1,0:T(8,128)(2,1)S(1)}, u32[]{:S(2)}, u32[]{:S(2)}) collective-permute-start(bf16[512,1024]{1,0:T(8,128)(2,1)S(1)} %constant_dynamic-slice_fusion), channel_id=1, source_target_pairs={{0,16},{4,20},{8,24},{12,28},{16,32},{20,36},{24,40},{28,44},{32,4... | collective-permute-start | bytes 3145736 | tf_op jit(solution)/shard_map/ppermute | solution.py:14
  88.1 56.9 %collective-permute-start.1 = (bf16[512,1024]{1,0:T(8,128)(2,1)S(1)}, bf16[512,1024]{1,0:T(8,128)(2,1)S(1)}, u32[]{:S(2)}, u32[]{:S(2)}) collective-permute-start(bf16[512,1024]{1,0:T(8,128)(2,1)S(1)} %constant_dynamic-slice_fusion), channel_id=1, source_target_pairs={{0,4},{4,8},{8,12},{12,16},{16,20},{20,24},{24,28},{28,32},{32,36}... | collective-permute-start | bytes 3145736 | tf_op jit(solution)/shard_map/ppermute | solution.py:14
  136.8 8.2 %collective-permute-start = (s32[512]{0:T(512)S(1)}, s32[512]{0:T(512)S(1)}, u32[]{:S(2)}, u32[]{:S(2)}) collective-permute-start(s32[512]{0:T(512)S(1)} %dynamic_slice.6), channel_id=1, source_target_pairs={{0,4},{4,8},{8,12},{12,16},{16,20},{20,24},{24,28},{28,32},{32,36}... | collective-permute-start | bytes 6152 | tf_op jit(solution)/shard_map/ppermute | solution.py:14
where the time goes:
time: 165 us; the launch traced here: 164 us
  waiting for transfers between devices  102 us (62%)
  starting transfers between devices  23.4 us (14%)
  matrix products  20 us (12%)
  blocking collectives  11.2 us (7%)
  other arithmetic  4.24 us (3%)
  local copies, waits for them, and re-layouts  2.91 us (2%)
    ppermute x8, waiting for transfers between devices, shifted(): return lax.ppermute(block, axis, route)  102 us
    ppermute x8, starting transfers between devices, shifted(): return lax.ppermute(block, axis, route)  23.4 us
    dot_general x5, matrix products, compare(): lax.dot_general(queries, keys, (((1,), (1,)), ((), ())), preferred_elemen...  20 us
    pmax x1, blocking collectives, local(): merged = lax.pmax(best_sim, 'rep')  11.2 us
  transfers between devices with their start and end apart: 8, of which 3 were waited for; matrix products, arithmetic and copies ran while one was open for 10% of the time, Pallas kernels for 0%

commit v1 on v0

v1 whole, which is shorter than its diff:
```python
import functools

import jax
import jax.numpy as jnp
from jax import lax
from jax.experimental import pallas as pl
from jax.experimental.pallas import tpu as pltpu
from jax.sharding import PartitionSpec as P

MESH = pl.DeviceIdType.MESH
NT = (((1,), (1,)), ((), ()))
BLOCK = 128
SUB = 32
STEPS = 4
PER = BLOCK // SUB
PIECES = STEPS * PER
WINDOW = 4
LAG = 2

OWN = 0
KEYS = 2048
KEY_STEP = 3 * BLOCK
QRY = KEYS + STEPS * KEY_STEP
SIDE = QRY + STEPS * 2 * BLOCK
TOTAL = SIDE + STEPS * 2 * BLOCK

Y_KEY, Y_QRY, X_KEY, X_QRY, S_KEY, S_QRY_A, S_QRY_X, MISC = range(8)


def kernel(shards, emb, labels, out, buf, klab, qlab, acc, lab, res, got_t, got_c, got_r, load_sem, send, recv):
    shard = lax.axis_index("shard")
    rep = lax.axis_index("rep")
    core = lax.rem(shard, 2)
    other = 1 - core
    chip2 = shard - core
    ahead = lax.rem(chip2 + 2, shards)
    behind = lax.rem(chip2 + shards - 2, shards)
    x_key = rep + 1 - 2 * lax.rem(rep, 2)
    x_qry = 3 - rep
    fwd, fwd_c = (ahead + core, rep), (ahead + other, rep)
    bwd, bwd_c = (behind + core, rep), (behind + other, rep)
    sib = (chip2 + other, rep)
    across = [(shard, lax.rem(rep + d, 4)) for d in (1, 2, 3)]

    def copy(src, dst, kind, index, device):
        return pltpu.make_async_remote_copy(
            src_ref=src,
            dst_ref=dst,
            send_sem=send.at[kind, index],
            recv_sem=recv.at[kind, index],
            device_id=device,
            device_id_type=MESH,
        )

    def rows(start, count):
        return pl.ds(pl.multiple_of(start, SUB), count)

    def at(start, count=SUB):
        return buf.at[rows(start, count)]

    def key_step(q):
        return STEPS - 1 - q // PER

    def key_slot(q, slot):
        return KEYS + key_step(q) * KEY_STEP + slot * BLOCK + (q % PER) * SUB

    def qry_slot(base, q, slot):
        return base + (q // PER) * 2 * BLOCK + slot * BLOCK + (q % PER) * SUB

    def y_key(q):
        src = (4 * key_step(q) + rep) * BLOCK + (q % PER) * SUB
        return copy(at(src), at(key_slot(q, 1)), Y_KEY, q, fwd)

    def y_qry(q):
        src = (4 * (q // PER) + rep) * BLOCK + (q % PER) * SUB
        return copy(at(src), at(qry_slot(QRY, q, 0)), Y_QRY, q, bwd)

    def s_key(q):
        return copy(at(key_slot(q, 1)), at(key_slot(q, 0)), S_KEY, q, sib)

    def xk(q):
        return copy(at(key_slot(q, 1)), at(key_slot(q, 2)), X_KEY, q, (shard, x_key))

    def xq(q):
        return copy(at(qry_slot(QRY, q, 0)), at(qry_slot(QRY, q, 1)), X_QRY, q, (shard, x_qry))

    def s_qry(q, slot):
        kind = (S_QRY_A, S_QRY_X)[slot]
        return copy(at(qry_slot(QRY, q, slot)), at(qry_slot(SIDE, q, slot)), kind, q, sib)

    def label_copies():
        return [copy(labels, lab.at[i], MISC, i, d) for i, d in enumerate((fwd, fwd_c, bwd, bwd_c, sib))]

    def side_block(j):
        return copy(at((4 * j + rep) * BLOCK, BLOCK), at(SIDE + j * BLOCK, BLOCK), MISC, 5 + j, sib)

    def load(b, i):
        r = rows(b * BLOCK, BLOCK)
        return pltpu.make_async_copy(emb.at[r], buf.at[r], load_sem.at[i])

    mine = [4 * j + rep for j in (3, 0, 2, 1)]
    rest = [4 * j + lax.rem(rep + o, 4) for j in range(4) for o in (1, 2, 3)]
    order = mine + rest
    for i, b in enumerate(order):
        load(b, i).start()

    barrier = pltpu.get_barrier_semaphore()
    for device in [fwd, fwd_c, bwd, bwd_c, sib] + across:
        pl.semaphore_signal(barrier, inc=1, device_id=device, device_id_type=MESH)

    def normalize(b):
        @pl.loop(0, BLOCK // 32)
        def _(i):
            r = rows(b * BLOCK + i * 32, 32)
            values = buf[r, :].astype(jnp.float32)
            inverse = lax.rsqrt(jnp.mean(values * values, axis=1, keepdims=True) + 1e-06)
            buf[r, :] = (values * inverse * (1.0 / 32.0)).astype(jnp.bfloat16)

    for i in range(2):
        load(order[i], i).wait()
        normalize(order[i])
    pl.semaphore_wait(barrier, 8)
    for q in range(WINDOW):
        y_key(q).start()
        y_qry(q).start()
    for c in label_copies():
        c.start()
    for i in range(2, 4):
        load(order[i], i).wait()
        normalize(order[i])

    @pl.when(core == 1)
    def _():
        for j in range(4):
            side_block(j).start()

    for i in range(4, 16):
        load(order[i], i).wait()
        normalize(order[i])

    acc[...] = jnp.full_like(acc, -1.0)
    res[...] = jnp.full_like(res, -1.0)
    for c in label_copies():
        c.wait_recv()

    def column(row, start):
        wide = jnp.broadcast_to(row, (BLOCK, BLOCK))
        klab[pl.ds(start, BLOCK), :] = wide.T

    def lab_row(i, r):
        return lab[i, pl.ds(r, 1), :]

    qlab[0:16, :] = labels[...]
    for b in range(16):
        column(labels[b:b + 1, :], b * BLOCK)
    for j in range(4):
        a = 4 * j + rep
        column(lab_row(1, a), KEYS + j * KEY_STEP)
        column(lab_row(0, a), KEYS + j * KEY_STEP + BLOCK)
        column(lab_row(0, 4 * j + x_key), KEYS + j * KEY_STEP + 2 * BLOCK)
        qlab[QRY // BLOCK + 2 * j:QRY // BLOCK + 2 * j + 1, :] = lab_row(2, a)
        qlab[QRY // BLOCK + 2 * j + 1:QRY // BLOCK + 2 * j + 2, :] = lab_row(2, 4 * j + x_qry)

    @pl.when(core == 1)
    def _():
        for j in range(4):
            s = SIDE // BLOCK + 2 * j
            qlab[s:s + 1, :] = lab_row(3, 4 * j + rep)
            qlab[s + 1:s + 2, :] = lab_row(3, 4 * j + x_qry)

    @pl.when(core == 0)
    def _():
        for j in range(4):
            qlab[SIDE // BLOCK + j:SIDE // BLOCK + j + 1, :] = lab_row(4, 4 * j + rep)

    def tile(key, qry, causal=False):
        key = pl.multiple_of(key, BLOCK)
        scores = lax.dot_general(
            buf[pl.ds(key, 256), :], buf[rows(qry, 256), :], NT, preferred_element_type=jnp.float32
        )
        lanes = klab[pl.ds(key, 256), :]
        for g in range(2):
            b = qry // BLOCK + g
            keep = lanes == qlab[pl.ds(b, 1), :]
            if causal:
                key_pos = key + lax.broadcasted_iota(jnp.int32, (256, BLOCK), 0)
                qry_pos = qry + g * BLOCK + lax.broadcasted_iota(jnp.int32, (256, BLOCK), 1)
                keep = keep & (key_pos < qry_pos)
            best = jnp.where(keep, scores[:, g * BLOCK:(g + 1) * BLOCK], jnp.float32(-1.0))
            best = jnp.max(best.reshape(32, 8, BLOCK), axis=0)
            a = pl.ds(pl.multiple_of(b * 8, 8), 8)
            acc[a, :] = jnp.maximum(acc[a, :], best)

    def key_tile(j):
        return KEYS + j * KEY_STEP

    def own_triangle(first):
        @pl.loop(first, 8)
        def _(t):
            tile(first * 256, t * 256, causal=True)

    def cross(lo, hi):
        @pl.when(core == 0)
        def _():
            @pl.loop(lo, hi)
            def _(k):
                for t in range(2):
                    tile(k * 256, SIDE + t * 256)

    def near(j, lo, hi):
        for t in range(lo, hi):
            tile(key_tile(j), OWN + t * 256)

    def far(s):
        j = STEPS - 1 - s
        key = key_tile(j) + BLOCK
        for t in range(0, min(s, j) + 1):
            tile(key, QRY + t * 256)
        for k in range(max(s, j + 1), STEPS):
            tile(key_tile(k) + BLOCK, QRY + s * 256)

        @pl.when(core == 1)
        def _():
            for t in range(0, s + 1):
                tile(key, SIDE + t * 256)
            for k in range(j + 1, STEPS):
                tile(key_tile(k) + BLOCK, SIDE + s * 256)

    def relay(q):
        xq(q).wait_recv()

        @pl.when(core == 0)
        def _():
            s_qry(q, 1).start()

    def service(q):
        y_key(q).wait_recv()
        xk(q).start()
        s_key(q).start()
        y_qry(q).wait_recv()
        xq(q).start()

        @pl.when(core == 0)
        def _():
            s_qry(q, 0).start()

        if q + WINDOW < PIECES:
            y_key(q + WINDOW).start()
            y_qry(q + WINDOW).start()
        if q >= LAG:
            relay(q - LAG)

    def near_ready(s):
        for q in range(PER * s, PER * s + PER):
            s_key(q).wait_recv()

    def far_ready(s):
        for q in range(PER * s, PER * s + PER):
            xk(q).wait_recv()

        @pl.when(core == 1)
        def _():
            for q in range(PER * s, PER * s + PER):
                s_qry(q, 0).wait_recv()
                s_qry(q, 1).wait_recv()

    for q in range(PIECES):
        service(q)
        s, u = q // PER - 1, q % PER
        if q == 0:
            own_triangle(rep)
        elif q == 1:
            own_triangle(7 - rep)

            @pl.when(core == 0)
            def _():
                for j in range(4):
                    side_block(j).wait_recv()
        elif q == 2:
            cross(0, 4)
        elif q == 3:
            cross(4, 8)
            r = SIDE // BLOCK

            @pl.when(core == 0)
            def _():
                for j in range(4):
                    b = (r + j) * 8
                    res[24 + j:25 + j, :] = jnp.max(acc[b:b + 8, :], axis=0, keepdims=True)
                copy(res.at[24:32], got_c, MISC, 9, sib).start()
        else:
            if u == 0:
                near_ready(s)
            near(STEPS - 1 - s, 2 * u, 2 * u + 2)
            if u == 3:
                far_ready(s)
                far(s)

    s = STEPS - 1
    near_ready(s)
    for q in range(PIECES - LAG, PIECES):
        relay(q)
    near(STEPS - 1 - s, 0, 8)
    far_ready(s)
    far(s)

    def reduce_into(dst, block, count):
        for i in range(count):
            b = (block + i) * 8
            res[dst + i:dst + i + 1, :] = jnp.max(acc[b:b + 8, :], axis=0, keepdims=True)

    reduce_into(16, QRY // BLOCK, 8)
    t_same = copy(res.at[16:24], got_t.at[0], MISC, 10, fwd)
    t_same.start()
    t_cross = copy(res.at[24:32], got_t.at[1], MISC, 11, fwd_c)
    c_cross = copy(res.at[24:32], got_c, MISC, 9, sib)

    @pl.when(core == 1)
    def _():
        reduce_into(24, SIDE // BLOCK, 8)
        t_cross.start()

    reduce_into(0, 0, 16)

    def merge(value, b):
        r = pl.ds(b, 1)
        res[r, :] = jnp.maximum(res[r, :], value)

    @pl.when(core == 1)
    def _():
        c_cross.wait_recv()
        for j in range(4):
            merge(got_c[j:j + 1, :], 4 * j + rep)

    def merge_t(i):
        for j in range(4):
            merge(got_t[i, 2 * j:2 * j + 1, :], 4 * j + rep)
            merge(got_t[i, 2 * j + 1:2 * j + 2, :], 4 * j + x_qry)

    t_same.wait_recv()
    merge_t(0)

    @pl.when(core == 0)
    def _():
        t_cross.wait_recv()
        merge_t(1)

    spread = [copy(res.at[0:16], got_r.at[i], MISC, 12 + i, across[i]) for i in range(3)]
    for c in spread:
        c.start()
    for c in spread:
        c.wait_recv()
    out[...] = jnp.maximum(jnp.maximum(res[0:16, :], got_r[0]), jnp.maximum(got_r[1], got_r[2]))

    for q in range(PIECES):
        for c in (y_key(q), y_qry(q), xk(q), xq(q), s_key(q)):
            c.wait_send()
    for c in label_copies() + spread + [t_same]:
        c.wait_send()

    @pl.when(core == 0)
    def _():
        for q in range(PIECES):
            s_qry(q, 0).wait_send()
            s_qry(q, 1).wait_send()
        c_cross.wait_send()

    @pl.when(core == 1)
    def _():
        for j in range(4):
            side_block(j).wait_send()
        t_cross.wait_send()


def solution(mesh):
    shards = mesh.shape["shard"]

    def local(embeddings, labels):
        best = pl.pallas_call(
            functools.partial(kernel, shards),
            out_shape=jax.ShapeDtypeStruct((16, 128), jnp.float32),
            in_specs=[pl.BlockSpec(memory_space=pl.ANY), pl.BlockSpec(memory_space=pltpu.VMEM)],
            out_specs=pl.BlockSpec(memory_space=pltpu.VMEM),
            scratch_shapes=[
                pltpu.VMEM((TOTAL, 1024), jnp.bfloat16),
                pltpu.VMEM((QRY, BLOCK), jnp.int32),
                pltpu.VMEM((TOTAL // BLOCK, BLOCK), jnp.int32),
                pltpu.VMEM((TOTAL // BLOCK * 8, BLOCK), jnp.float32),
                pltpu.VMEM((5, 16, BLOCK), jnp.int32),
                pltpu.VMEM((32, BLOCK), jnp.float32),
                pltpu.VMEM((2, 8, BLOCK), jnp.float32),
                pltpu.VMEM((8, BLOCK), jnp.float32),
                pltpu.VMEM((3, 16, BLOCK), jnp.float32),
                pltpu.SemaphoreType.DMA((16,)),
                pltpu.SemaphoreType.DMA((8, 16)),
                pltpu.SemaphoreType.DMA((8, 16)),
            ],
            compiler_params=pltpu.CompilerParams(
                collective_id=0, has_side_effects=True, vmem_limit_bytes=56 * 2**20
            ),
        )(embeddings, labels.reshape(16, 128))
        return best.reshape(2048)

    placed = (P("shard", None), P("shard"))
    return jax.shard_map(local, mesh=mesh, in_specs=placed, out_specs=P("shard"), check_vma=False)
```

time: 165 us -> 69.5 us (0.42)
  the two profiles are of different devices: /device:TPU:256 before, /device:TPU:1 now
where the time goes in v1:
time: 69.5 us; the launch traced here: 69.3 us
  Pallas kernels  68 us (98%)
  local copies, waits for them, and re-layouts  1.3 us (2%)
    pallas_call x1, Pallas kernels, local(): pl.pallas_call(functools.partial(kernel, shards), out_shape=jax.ShapeDtyp...  68 us

profile of v1, /device:TPU:1, one launch (start us, length us, event | category | flops | bytes accessed | tf_op | source)
XLA Modules:
  0.0 69.3 jit_solution(367151801878362046)
XLA Ops:
  0.0 68.0 %shard_map.28 = f32[16,128]{1,0:T(8,128)} custom-call(bf16[2048,1024]{1,0:T(8,128)(2,1)} %emb.1, s32[16,128]{1,0:T(8,128)} %bitcast.3), custom_call_target="tpu_custom_call" | custom-call | tf_op jit(solution)/shard_map/pallas_call | solution.py:379
  68.0 1.3 %copy.4 = f32[2048]{0:T(1024)} copy(f32[2048]{0:T(1024)} %bitcast.2) | data formatting | bytes 16384

commit v2 on v0

v2 whole, which is shorter than its diff:
```python
import functools

import jax
import jax.numpy as jnp
from jax import lax
from jax.experimental import pallas as pl
from jax.experimental.pallas import tpu as pltpu
from jax.sharding import PartitionSpec as P

MESH = pl.DeviceIdType.MESH
NT = (((1,), (1,)), ((), ()))
BLOCK = 128
SUB = 16
STEPS = 4
PER = BLOCK // SUB
PIECES = STEPS * PER
WINDOW = 6
DELAY = 8
LAG = 6

OWN = 0
KEYS = 2048
KEY_STEP = 3 * BLOCK
QRY = KEYS + STEPS * KEY_STEP
SIDE = QRY + STEPS * 2 * BLOCK
TOTAL = SIDE + STEPS * 2 * BLOCK

Y_KEY, Y_QRY, X_QRY, MISC = range(4)
X_KEY, S_KEY, S_QRY_A, S_QRY_X = range(4)


def scope(name):
    return jax.named_scope(name)


def kernel(shards, emb, labels, out, buf, klab, qlab, acc, lab, res, got_t, got_s, got_c, got_r,
           load_sem, piece_sem, step_sem, y_sent, sent_sem, misc_sent, hello):
    shard = lax.axis_index("shard")
    rep = lax.axis_index("rep")
    core = lax.rem(shard, 2)
    other = 1 - core
    chip2 = shard - core
    has_prev = chip2 > 0
    has_next = chip2 < shards - 2
    mid = has_prev & has_next
    sends_qry = chip2 > 2
    ahead = lax.rem(chip2 + 2, shards)
    behind = lax.rem(chip2 + shards - 2, shards)
    x_key = rep + 1 - 2 * lax.rem(rep, 2)
    x_qry = 3 - rep
    fwd, fwd_c = (ahead + core, rep), (ahead + other, rep)
    bwd, bwd_c = (behind + core, rep), (behind + other, rep)
    sib = (chip2 + other, rep)
    across = [(shard, lax.rem(rep + d, 4)) for d in (1, 2, 3)]
    first = (shard == 0) & (rep == 0)
    greeted = (shard == 0) & (rep > 0) | (shard == 1) & (rep == 0)

    def remote(src, dst, sent, got, device):
        return pltpu.make_async_remote_copy(
            src_ref=src, dst_ref=dst, send_sem=sent, recv_sem=got, device_id=device, device_id_type=MESH
        )

    def rows(start, count):
        return pl.ds(pl.multiple_of(start, SUB), count)

    def at(start, count=SUB):
        return buf.at[rows(start, count)]

    def key_step(q):
        return STEPS - 1 - q // PER

    def key_slot(q, slot):
        return KEYS + key_step(q) * KEY_STEP + slot * BLOCK + (q % PER) * SUB

    def qry_slot(base, q, slot):
        return base + (q // PER) * 2 * BLOCK + slot * BLOCK + (q % PER) * SUB

    def y_key(q):
        src = (4 * key_step(q) + rep) * BLOCK + (q % PER) * SUB
        return remote(at(src), at(key_slot(q, 1)), y_sent.at[0, q], piece_sem.at[Y_KEY, q], fwd)

    def y_qry(q):
        src = (4 * (q // PER) + rep) * BLOCK + (q % PER) * SUB
        return remote(at(src), at(qry_slot(QRY, q, 0)), y_sent.at[1, q], piece_sem.at[Y_QRY, q], bwd)

    def xq(q):
        dst = at(qry_slot(QRY, q, 1))
        return remote(at(qry_slot(QRY, q, 0)), dst, sent_sem.at[2], piece_sem.at[X_QRY, q], (shard, x_qry))

    def xk(q):
        dst = at(key_slot(q, 2))
        return remote(at(key_slot(q, 1)), dst, sent_sem.at[3], step_sem.at[X_KEY, q // PER], (shard, x_key))

    def s_key(q):
        return remote(at(key_slot(q, 1)), at(key_slot(q, 0)), sent_sem.at[4], step_sem.at[S_KEY, q // PER], sib)

    def s_qry(q, slot):
        src, dst = at(qry_slot(QRY, q, slot)), at(qry_slot(SIDE, q, slot))
        return remote(src, dst, sent_sem.at[5 + slot], step_sem.at[S_QRY_A + slot, q // PER], sib)

    def whole_step(kind, s):
        remote(at(0, BLOCK), at(0, BLOCK), sent_sem.at[0], step_sem.at[kind, s], sib).wait_recv()

    def all_sent(i):
        remote(at(0, PIECES * SUB), at(0, PIECES * SUB), sent_sem.at[i], step_sem.at[0, 0], sib).wait_send()

    def misc(src, dst, index, device):
        return remote(src, dst, misc_sent.at[index], piece_sem.at[MISC, index], device)

    def label_fwd():
        return [misc(labels, lab.at[i], i, d) for i, d in enumerate((fwd, fwd_c))]

    def label_bwd():
        return [misc(labels, lab.at[2 + i], 2 + i, d) for i, d in enumerate((bwd, bwd_c))]

    def label_sib():
        return misc(labels, lab.at[4], 4, sib)

    def side_block(j):
        return misc(at((4 * j + rep) * BLOCK, BLOCK), at(SIDE + j * BLOCK, BLOCK), 5 + j, sib)

    def cross_result():
        return misc(res.at[24:32], got_c, 9, sib)

    def spread(i):
        return misc(res.at[0:16], got_r.at[i], 10 + i, across[i])

    def qry_result(x):
        return remote(res.at[16:24], got_t.at[rep], misc_sent.at[13 + x], piece_sem.at[MISC, 13 + rep], (ahead + core, x))

    def side_result(x):
        return remote(res.at[24:32], got_s.at[rep], misc_sent.at[17 + x], piece_sem.at[MISC, 17 + rep], (ahead, x))

    def from_prev(kind, x):
        i, dst = ((13, got_t), (17, got_s))[kind]
        return remote(res.at[16:24], dst.at[x], misc_sent.at[i], piece_sem.at[MISC, i + x], fwd)

    def load(b, i):
        r = rows(b * BLOCK, BLOCK)
        return pltpu.make_async_copy(emb.at[r], buf.at[r], load_sem.at[i])

    mine = [4 * j + rep for j in (3, 0, 2, 1)]
    rest = [4 * j + lax.rem(rep + o, 4) for j in range(4) for o in (1, 2, 3)]
    order = mine + rest
    for i, b in enumerate(order):
        load(b, i).start()

    barrier = pltpu.get_barrier_semaphore()

    def greet(device):
        pl.semaphore_signal(barrier, inc=1, device_id=device, device_id_type=MESH)

    @pl.when(has_prev)
    def _():
        for x in range(4):
            for h in range(2):
                greet((behind + h, x))

    @pl.when(mid)
    def _():
        greet(fwd)
        greet(fwd_c)

    @pl.when(jnp.logical_not(first))
    def _():
        for device in [sib] + across:
            greet(device)

    def normalize(b):
        r = rows(b * BLOCK, BLOCK)
        total = jnp.zeros((BLOCK, 128), jnp.float32)
        for c in range(8):
            v = buf[r, c * 128:(c + 1) * 128].astype(jnp.float32)
            total = total + v * v
        mean = jnp.sum(total, axis=1, keepdims=True) * (1.0 / 1024.0)
        scale = jnp.broadcast_to(lax.rsqrt(mean + 1e-06), (BLOCK, 128))
        for c in range(8):
            v = buf[r, c * 128:(c + 1) * 128].astype(jnp.float32)
            buf[r, c * 128:(c + 1) * 128] = (v * scale * (1.0 / 32.0)).astype(jnp.bfloat16)

    def prepare(lo, hi):
        for i in range(lo, hi):
            load(order[i], i).wait()
            normalize(order[i])

    with scope("norm_first"):
        prepare(0, 2)
    with scope("barrier"):
        one = lambda flag: jnp.where(flag, 1, 0)
        pl.semaphore_wait(barrier, 8 * one(has_next) + 2 * one(sends_qry) + 4 - one(greeted))

        @pl.when(first)
        def _():
            for device in [sib] + across:
                pl.semaphore_signal(hello, inc=1, device_id=device, device_id_type=MESH)

    @pl.when(has_next)
    def _():
        for c in label_fwd():
            c.start()

    @pl.when(sends_qry)
    def _():
        for c in label_bwd():
            c.start()

    late_sib = first | (shard == 1) & (rep == 0)

    @pl.when(jnp.logical_not(late_sib))
    def _():
        label_sib().start()

    def send_y(q):
        @pl.when(mid if q >= WINDOW else has_next)
        def _():
            if q >= WINDOW:
                y_key(q - WINDOW).wait_send()
            y_key(q).start()

        @pl.when(sends_qry)
        def _():
            if q >= WINDOW:
                y_qry(q - WINDOW).wait_send()
            y_qry(q).start()

    for q in range(WINDOW):
        send_y(q)
    with scope("norm_mine"):
        prepare(2, 4)

    @pl.when((core == 1) & jnp.logical_not(late_sib))
    def _():
        for j in range(4):
            side_block(j).start()

    @pl.when(chip2 == 0)
    def _():
        for q in range(WINDOW, PIECES):
            y_key(q).start()

    with scope("norm_rest"):
        prepare(4, 16)

    def column(row, start):
        wide = jnp.broadcast_to(row, (BLOCK, BLOCK))
        klab[pl.ds(start, BLOCK), :] = wide.T

    def lab_row(i, r):
        return lab[i, pl.ds(r, 1), :]

    def own_labels():
        acc[...] = jnp.full_like(acc, -1.0)
        res[...] = jnp.full_like(res, -1.0)
        qlab[0:16, :] = labels[...]
        for b in range(16):
            column(labels[b:b + 1, :], b * BLOCK)

    def far_labels():
        @pl.when(has_prev)
        def _():
            for c in label_fwd():
                c.wait_recv()
            for j in range(4):
                a = 4 * j + rep
                column(lab_row(1, a), KEYS + j * KEY_STEP)
                column(lab_row(0, a), KEYS + j * KEY_STEP + BLOCK)
                column(lab_row(0, 4 * j + x_key), KEYS + j * KEY_STEP + 2 * BLOCK)

        @pl.when(mid)
        def _():
            for c in label_bwd():
                c.wait_recv()
            for j in range(4):
                s = QRY // BLOCK + 2 * j
                qlab[s:s + 1, :] = lab_row(2, 4 * j + rep)
                qlab[s + 1:s + 2, :] = lab_row(2, 4 * j + x_qry)

            @pl.when(core == 1)
            def _():
                for j in range(4):
                    s = SIDE // BLOCK + 2 * j
                    qlab[s:s + 1, :] = lab_row(3, 4 * j + rep)
                    qlab[s + 1:s + 2, :] = lab_row(3, 4 * j + x_qry)

    def sib_ready():
        @pl.when(late_sib)
        def _():
            @pl.when(core == 1)
            def _():
                pl.semaphore_wait(hello, 1)
                for j in range(4):
                    side_block(j).start()
            label_sib().start()

        label_sib().wait_recv()

        @pl.when(core == 0)
        def _():
            for j in range(4):
                qlab[SIDE // BLOCK + j:SIDE // BLOCK + j + 1, :] = lab_row(4, 4 * j + rep)
                side_block(j).wait_recv()

    def tile(key, qry, causal=False):
        key = pl.multiple_of(key, BLOCK)
        scores = lax.dot_general(
            buf[pl.ds(key, 256), :], buf[rows(qry, 256), :], NT, preferred_element_type=jnp.float32
        )
        lanes = klab[pl.ds(key, 256), :]
        for g in range(2):
            b = qry // BLOCK + g
            keep = lanes == qlab[pl.ds(b, 1), :]
            if causal:
                key_pos = key + lax.broadcasted_iota(jnp.int32, (256, BLOCK), 0)
                qry_pos = qry + g * BLOCK + lax.broadcasted_iota(jnp.int32, (256, BLOCK), 1)
                keep = keep & (key_pos < qry_pos)
            best = jnp.where(keep, scores[:, g * BLOCK:(g + 1) * BLOCK], jnp.float32(-1.0))
            best = jnp.max(best.reshape(32, 8, BLOCK), axis=0)
            a = pl.ds(pl.multiple_of(b * 8, 8), 8)
            acc[a, :] = jnp.maximum(acc[a, :], best)

    def key_tile(j):
        return KEYS + j * KEY_STEP

    def own_triangle(lo, hi):
        for i in range(lo, hi):
            low = i < 8 - rep
            key = jnp.where(low, rep, 7 - rep)
            qry = jnp.where(low, rep + i, i - 1)
            tile(key * 256, qry * 256, causal=True)

    def cross(lo, hi):
        @pl.when(core == 0)
        def _():
            for k in range(lo, hi):
                for t in range(2):
                    tile(k * 256, SIDE + t * 256)

    def best_rows(dst, block, count):
        for i in range(count):
            b = (block + i) * 8
            res[dst + i:dst + i + 1, :] = jnp.max(acc[b:b + 8, :], axis=0, keepdims=True)

    def cross_done():
        @pl.when(core == 0)
        def _():
            best_rows(24, SIDE // BLOCK, 4)
            cross_result().start()

    def near(s, lo, hi):
        @pl.when(has_prev)
        def _():
            if lo == 0:
                whole_step(S_KEY, s)
            for t in range(lo, hi):
                tile(key_tile(STEPS - 1 - s), OWN + t * 256)

    def far(s):
        j = STEPS - 1 - s

        @pl.when(mid)
        def _():
            whole_step(X_KEY, s)

            @pl.when(core == 1)
            def _():
                for q in range(s * PER, (s + 1) * PER):
                    xq(q).wait_recv()

            key = key_tile(j) + BLOCK
            for t in range(0, min(s, j) + 1):
                tile(key, QRY + t * 256)
            for k in range(max(s, j + 1), STEPS):
                tile(key_tile(k) + BLOCK, QRY + s * 256)

    def far_side(s):
        j = STEPS - 1 - s

        @pl.when(mid & (core == 1))
        def _():
            whole_step(S_QRY_A, s)
            whole_step(S_QRY_X, s)
            key = key_tile(j) + BLOCK
            for t in range(0, s + 1):
                tile(key, SIDE + t * 256)
            for k in range(j + 1, STEPS):
                tile(key_tile(k) + BLOCK, SIDE + s * 256)

    def relay(q):
        @pl.when(mid & (core == 0))
        def _():
            xq(q).wait_recv()
            s_qry(q, 1).start()

    def service(q):
        @pl.when(has_prev)
        def _():
            y_key(q).wait_recv()
            s_key(q).start()

        @pl.when(mid)
        def _():
            xk(q).start()
            y_qry(q).wait_recv()
            xq(q).start()

            @pl.when(core == 0)
            def _():
                s_qry(q, 0).start()

        if q >= LAG:
            relay(q - LAG)

    work = {q: [] for q in range(PIECES)}

    def plan(q, f, *a):
        work[q].append((f, a))

    plan(0, own_labels)
    plan(1, far_labels)
    for i in range(3):
        plan(2 + i, own_triangle, 3 * i, 3 * i + 3)
    plan(5, sib_ready)
    for i in range(4):
        plan(5 + i, cross, 2 * i, 2 * i + 2)
    plan(9, cross_done)
    for i in range(4):
        plan(10 + i, near, 0, 2 * i, 2 * i + 2)
        plan(17 + i, near, 1, 2 * i, 2 * i + 2)
    plan(25, near, 2, 0, 4)
    plan(26, near, 2, 4, 8)
    plan(15, far, 0)
    plan(21, far_side, 0)
    plan(23, far, 1)
    plan(27, far_side, 1)
    plan(29, far, 2)

    for q in range(WINDOW, DELAY):
        send_y(q)
    for q in range(PIECES):
        with scope("service%d" % q):
            if q + DELAY < PIECES:
                send_y(q + DELAY)
            service(q)
        with scope("work%d" % q):
            for f, a in work[q]:
                f(*a)

    with scope("tail_near"):
        for q in range(PIECES - LAG, PIECES - 2):
            relay(q)
        far_side(2)
        relay(PIECES - 2)
        near(3, 0, 4)
        relay(PIECES - 1)
        near(3, 4, 8)

    def merge(value, b):
        r = pl.ds(b, 1)
        res[r, :] = jnp.maximum(res[r, :], value)

    with scope("own_result"):
        best_rows(0, 0, 16)

        @pl.when(core == 1)
        def _():
            cross_result().wait_recv()
            for j in range(4):
                merge(got_c[j:j + 1, :], 4 * j + rep)

        @pl.when((core == 0) & greeted)
        def _():
            pl.semaphore_wait(hello, 1)

        for i in range(3):
            spread(i).start()

    with scope("tail_far"):
        far(3)

        @pl.when(mid)
        def _():
            best_rows(16, QRY // BLOCK, 8)
            for x in range(4):
                qry_result(x).start()

    with scope("tail_side"):
        far_side(3)

        @pl.when(mid & (core == 1))
        def _():
            best_rows(24, SIDE // BLOCK, 8)
            for x in range(4):
                side_result(x).start()

    with scope("spread_wait"):
        for i in range(3):
            spread(i).wait_recv()
        out[...] = jnp.maximum(jnp.maximum(res[0:16, :], got_r[0]), jnp.maximum(got_r[1], got_r[2]))

    def take(got):
        for r in range(4):
            for j in range(4):
                b = 4 * j + r
                best = jnp.maximum(got[r, 2 * j:2 * j + 1, :], got[3 - r, 2 * j + 1:2 * j + 2, :])
                out[b:b + 1, :] = jnp.maximum(out[b:b + 1, :], best)

    with scope("result_wait"):
        @pl.when(sends_qry)
        def _():
            for x in range(4):
                from_prev(0, x).wait_recv()
            take(got_t)

            @pl.when(core == 0)
            def _():
                for x in range(4):
                    from_prev(1, x).wait_recv()
                take(got_s)

    with scope("sent"):
        for i in range(3):
            spread(i).wait_send()
        label_sib().wait_send()

        @pl.when(has_next)
        def _():
            @pl.when(chip2 == 0)
            def _():
                for q in range(PIECES - WINDOW):
                    y_key(q).wait_send()
            for q in range(PIECES - WINDOW, PIECES):
                y_key(q).wait_send()
            for c in label_fwd():
                c.wait_send()

        @pl.when(sends_qry)
        def _():
            for q in range(PIECES - WINDOW, PIECES):
                y_qry(q).wait_send()
            for c in label_bwd():
                c.wait_send()

        @pl.when(has_prev)
        def _():
            all_sent(4)

        @pl.when(mid)
        def _():
            all_sent(2)
            all_sent(3)
            for x in range(4):
                qry_result(x).wait_send()

            @pl.when(core == 0)
            def _():
                all_sent(5)
                all_sent(6)

            @pl.when(core == 1)
            def _():
                for x in range(4):
                    side_result(x).wait_send()

        @pl.when(core == 0)
        def _():
            cross_result().wait_send()

        @pl.when(core == 1)
        def _():
            for j in range(4):
                side_block(j).wait_send()


def solution(mesh):
    shards = mesh.shape["shard"]

    def local(embeddings, labels):
        best = pl.pallas_call(
            functools.partial(kernel, shards),
            out_shape=jax.ShapeDtypeStruct((16, 128), jnp.float32),
            in_specs=[pl.BlockSpec(memory_space=pl.ANY), pl.BlockSpec(memory_space=pltpu.VMEM)],
            out_specs=pl.BlockSpec(memory_space=pltpu.VMEM),
            scratch_shapes=[
                pltpu.VMEM((TOTAL, 1024), jnp.bfloat16),
                pltpu.VMEM((QRY, BLOCK), jnp.int32),
                pltpu.VMEM((TOTAL // BLOCK, BLOCK), jnp.int32),
                pltpu.VMEM((TOTAL // BLOCK * 8, BLOCK), jnp.float32),
                pltpu.VMEM((5, 16, BLOCK), jnp.int32),
                pltpu.VMEM((32, BLOCK), jnp.float32),
                pltpu.VMEM((4, 8, BLOCK), jnp.float32),
                pltpu.VMEM((4, 8, BLOCK), jnp.float32),
                pltpu.VMEM((8, BLOCK), jnp.float32),
                pltpu.VMEM((3, 16, BLOCK), jnp.float32),
                pltpu.SemaphoreType.DMA((16,)),
                pltpu.SemaphoreType.DMA((4, 32)),
                pltpu.SemaphoreType.DMA((4, STEPS)),
                pltpu.SemaphoreType.DMA((2, 32)),
                pltpu.SemaphoreType.DMA((7,)),
                pltpu.SemaphoreType.DMA((21,)),
                pltpu.SemaphoreType.REGULAR,
            ],
            compiler_params=pltpu.CompilerParams(
                collective_id=0, has_side_effects=True, vmem_limit_bytes=56 * 2**20
            ),
        )(embeddings, labels.reshape(16, 128))
        return best.reshape(2048)

    placed = (P("shard", None), P("shard"))
    return jax.shard_map(local, mesh=mesh, in_specs=placed, out_specs=P("shard"), check_vma=False)
```

time: 165 us -> 48.1 us (0.29)
  waiting for transfers between devices: 102 us -> 0 us
  Pallas kernels: 0 us -> 46.6 us
  starting transfers between devices: 23.4 us -> 0 us
  matrix products: 20 us -> 0 us
  blocking collectives: 11.2 us -> 0 us
  other arithmetic: 4.24 us -> 0 us
    ppermute x8 -> x0, waiting for transfers between devices: 102 us -> none  [shifted(): return lax.ppermute(block, axis, route)]
    pallas_call x0 -> x1, Pallas kernels: none -> 46.6 us  [local(): pl.pallas_call(functools.partial(kernel, shards), out_shape=jax.ShapeDtyp...]
    ppermute x8 -> x0, starting transfers between devices: 23.4 us -> none  [shifted(): return lax.ppermute(block, axis, route)]
    dot_general x5 -> x0, matrix products: 20 us -> none  [compare(): lax.dot_general(queries, keys, (((1,), (1,)), ((), ())), preferred_elemen...]
    pmax x1 -> x0, blocking collectives: 11.2 us -> none  [local(): merged = lax.pmax(best_sim, 'rep')]
    reduce_sum x1 -> x0, other arithmetic: 3.08 us -> none  [normalize(): jnp.mean(as_float * as_float, axis=1, keepdims=True) + 1e-06]
  transfers between devices with their start and end apart: 8 -> 0, of which waited for: 3 -> 0; matrix products, arithmetic and copies ran while one was open for 10% -> 0% of each run, Pallas kernels for 0% -> 0%
where the time goes in v2:
time: 48.1 us; the launch traced here: 47.9 us
  Pallas kernels  46.6 us (97%)
  local copies, waits for them, and re-layouts  1.3 us (3%)
    pallas_call x1, Pallas kernels, local(): pl.pallas_call(functools.partial(kernel, shards), out_shape=jax.ShapeDtyp...  46.6 us
    unnamed x1, local copies, waits for them, and re-layouts  1.3 us

profile of v2, /device:TPU:256, one launch (start us, length us, event | category | flops | bytes accessed | tf_op | source)
XLA Modules:
  0.0 47.9 jit_solution(15197407895665272914)
XLA Ops:
  0.0 46.6 %shard_map.28 = f32[16,128]{1,0:T(8,128)} custom-call(bf16[2048,1024]{1,0:T(8,128)(2,1)} %emb.1, s32[16,128]{1,0:T(8,128)} %bitcast.3), custom_call_target="tpu_custom_call" | custom-call | tf_op jit(solution)/shard_map/pallas_call | solution.py:578
  46.6 1.3 %copy.4 = f32[2048]{0:T(1024)} copy(f32[2048]{0:T(1024)} %bitcast.2) | data formatting | bytes 16384

commit v3 on v2

--- a/solution.py
+++ b/solution.py
@@ -14,9 +14,10 @@
 STEPS = 4
 PER = BLOCK // SUB
 PIECES = STEPS * PER
-WINDOW = 6
+WINDOW = 8
 DELAY = 8
 LAG = 6
+DIRECT = 2
 
 OWN = 0
 KEYS = 2048
@@ -98,6 +99,10 @@
         src, dst = at(qry_slot(QRY, q, slot)), at(qry_slot(SIDE, q, slot))
         return remote(src, dst, sent_sem.at[5 + slot], step_sem.at[S_QRY_A + slot, q // PER], sib)
 
+    def xq_side(q):
+        dst = at(qry_slot(SIDE, q, 1))
+        return remote(at(qry_slot(QRY, q, 0)), dst, sent_sem.at[6], step_sem.at[S_QRY_X, q // PER], (chip2 + other, x_qry))
+
     def whole_step(kind, s):
         remote(at(0, BLOCK), at(0, BLOCK), sent_sem.at[0], step_sem.at[kind, s], sib).wait_recv()
 
@@ -142,8 +147,8 @@
     mine = [4 * j + rep for j in (3, 0, 2, 1)]
     rest = [4 * j + lax.rem(rep + o, 4) for j in range(4) for o in (1, 2, 3)]
     order = mine + rest
-    for i, b in enumerate(order):
-        load(b, i).start()
+    for i in range(4):
+        load(order[i], i).start()
 
     barrier = pltpu.get_barrier_semaphore()
 
@@ -160,6 +165,10 @@
     def _():
         greet(fwd)
         greet(fwd_c)
+
+        @pl.when(core == 1)
+        def _():
+            greet((chip2, x_qry))
 
     @pl.when(jnp.logical_not(first))
     def _():
@@ -187,7 +196,7 @@
         prepare(0, 2)
     with scope("barrier"):
         one = lambda flag: jnp.where(flag, 1, 0)
-        pl.semaphore_wait(barrier, 8 * one(has_next) + 2 * one(sends_qry) + 4 - one(greeted))
+        pl.semaphore_wait(barrier, 8 * one(has_next) + 2 * one(sends_qry) + 4 + one(mid & (core == 0)) - one(greeted))
 
         @pl.when(first)
         def _():
@@ -225,6 +234,8 @@
 
     for q in range(WINDOW):
         send_y(q)
+    for i in range(4, 16):
+        load(order[i], i).start()
     with scope("norm_mine"):
         prepare(2, 4)
 
@@ -389,7 +400,8 @@
         @pl.when(mid & (core == 0))
         def _():
             xq(q).wait_recv()
-            s_qry(q, 1).start()
+            if q < PIECES - DIRECT:
+                s_qry(q, 1).start()
 
     def service(q):
         @pl.when(has_prev)
@@ -405,6 +417,8 @@
 
             @pl.when(core == 0)
             def _():
+                if q >= PIECES - DIRECT:
+                    xq_side(q).start()
                 s_qry(q, 0).start()
 
         if q >= LAG:
@@ -418,20 +432,23 @@
     plan(0, own_labels)
     plan(1, far_labels)
     for i in range(3):
-        plan(2 + i, own_triangle, 3 * i, 3 * i + 3)
-    plan(5, sib_ready)
-    for i in range(4):
-        plan(5 + i, cross, 2 * i, 2 * i + 2)
-    plan(9, cross_done)
-    for i in range(4):
-        plan(10 + i, near, 0, 2 * i, 2 * i + 2)
-        plan(17 + i, near, 1, 2 * i, 2 * i + 2)
+        plan(2 + 2 * i, own_triangle, 3 * i, 3 * i + 3)
+    plan(7, sib_ready)
+    plan(8, cross, 0, 2)
+    plan(10, cross, 2, 4)
+    plan(11, near, 0, 0, 4)
+    plan(13, near, 0, 4, 8)
+    plan(14, cross, 4, 6)
+    plan(16, cross, 6, 8)
+    plan(17, far, 0)
+    plan(17, cross_done)
+    plan(18, near, 1, 0, 4)
+    plan(19, far_side, 0)
+    plan(20, near, 1, 4, 8)
+    plan(23, far, 1)
     plan(25, near, 2, 0, 4)
-    plan(26, near, 2, 4, 8)
-    plan(15, far, 0)
-    plan(21, far_side, 0)
-    plan(23, far, 1)
-    plan(27, far_side, 1)
+    plan(26, far_side, 1)
+    plan(27, near, 2, 4, 8)
     plan(29, far, 2)
 
     for q in range(WINDOW, DELAY):

time: 48.1 us -> 47.6 us (0.990)
  Pallas kernels: 46.6 us -> 46.1 us
    pallas_call x1, Pallas kernels: 46.6 us -> 46.1 us  [local(): pl.pallas_call(functools.partial(kernel, shards), out_shape=jax.ShapeDtyp...]
where the time goes in v3:
time: 47.6 us; the launch traced here: 47.4 us
  Pallas kernels  46.1 us (97%)
  local copies, waits for them, and re-layouts  1.3 us (3%)
    pallas_call x1, Pallas kernels, local(): pl.pallas_call(functools.partial(kernel, shards), out_shape=jax.ShapeDtyp...  46.1 us
    unnamed x1, local copies, waits for them, and re-layouts  1.3 us

profile of v3, /device:TPU:256, one launch (start us, length us, event | category | flops | bytes accessed | tf_op | source)
XLA Modules:
  0.0 47.4 jit_solution(17667840282467841994)
XLA Ops:
  0.0 46.1 %shard_map.28 = f32[16,128]{1,0:T(8,128)} custom-call(bf16[2048,1024]{1,0:T(8,128)(2,1)} %emb.1, s32[16,128]{1,0:T(8,128)} %bitcast.3), custom_call_target="tpu_custom_call" | custom-call | tf_op jit(solution)/shard_map/pallas_call | solution.py:595
  46.1 1.3 %copy.4 = f32[2048]{0:T(1024)} copy(f32[2048]{0:T(1024)} %bitcast.2) | data formatting | bytes 16384
